TPU v7x, 32 devices: a whole 2x2x4 slice. The times are simulated.
32 devices in a mesh: group: 4 (over z), expert: 8 (over y, x, core).
Axes of the slice: x: 2, y: 2, z: 4, core: 2. Of those that a mesh axis runs over, the one named last changes fastest.
Arguments:
- group_logits: float32 [4096, 4], P(('group', 'expert')), may hold values from -6 to 6
- expert_logits: float32 [4096, 32], P(('group', 'expert')), may hold values from -6 to 6
- expert_ids: int32 [4096, 2], P(('group', 'expert')), may hold values from 0 to 31, all different within a row; in each aligned block of 128 rows (0 to 127, 128 to 255, ...) at most 16 rows name the same one
- cotangent: bfloat16 [4096, 3584], P(('group', 'expert')), may hold values from -6 to 6
- hidden_saved: bfloat16 [32, 512, 1024], P(('group', 'expert')), may hold values from -0.1875 to 0.1875
- w_down: bfloat16 [32, 1024, 3584], P(('group', 'expert')), may hold values from -0.1875 to 0.1875
Outputs:
- hidden_grad: bfloat16 [32, 512, 1024], P(('group', 'expert'))
- d_group_logits: float32 [4096, 4], P(('group', 'expert'))
- d_expert_logits: float32 [4096, 32], P(('group', 'expert'))
Inputs may be any that keep to these rules, and one draw needn't show every extreme that they name: `expert_ids`: within the 128 tokens of one device no expert is named by more than 16 choices, a bound that some block reaches; the 2 experts of a token differ.
All inputs are finite; a program needn't handle non-finite values.
Results may differ from a plain program's by a relative error of at most 0.0045.
Values may be sent and summed in bfloat16 or wider, within the bound.
No kernel may reach another device: no remote copies, remote signals or barrier semaphores. Data moves between devices by JAX's collectives and lax.ppermute only.
A program may use at most 64 MiB of HBM per device.

v0:
```python
from functools import partial
import jax
import jax.numpy as jnp
from jax import lax
from jax.sharding import PartitionSpec as P

ITERS = 5
SOFTCAP = 4.0


def capped(logits):
    return jnp.exp(SOFTCAP * jnp.tanh(logits / SOFTCAP))


def squashing(logits):
    bounded = jnp.tanh(logits / SOFTCAP)
    return 1.0 - bounded * bounded


def balance_level(level_in, target, column_sum):
    scaled = level_in * (target / column_sum)
    return (scaled, jnp.sum(scaled, -1, keepdims=True))


def adjoint_local(out_grad, level_in, target, column_sum):
    scaled, row_total = balance_level(level_in, target, column_sum)
    level_out = scaled / row_total
    scaled_grad = (out_grad - jnp.sum(out_grad * level_out, -1, keepdims=True)) / row_total
    return (scaled_grad, jnp.sum(scaled_grad * level_in, 0))


def adjoint_finish(scaled_grad, inner, target, column_sum):
    return target / column_sum * (scaled_grad - inner / column_sum)


def balance_step(targets, current, unused):
    target_group, target_expert = targets
    group_in, expert_in = current
    group_cols, expert_cols = lax.psum(
        (jnp.sum(group_in, 0), jnp.sum(expert_in, 0)), ("group", "expert")
    )
    scaled_g, rowsum_g = balance_level(group_in, target_group, group_cols)
    scaled_e, rowsum_e = balance_level(expert_in, target_expert, expert_cols)
    return (
        (scaled_g / rowsum_g, scaled_e / rowsum_e),
        (group_in, expert_in, group_cols, expert_cols),
    )


def adjoint_step(targets, carried, stored_step):
    target_group, target_expert = targets
    grad_g, grad_e = carried
    group_in, expert_in, group_cols, expert_cols = stored_step
    scaled_g, inner_g = adjoint_local(grad_g, group_in, target_group, group_cols)
    scaled_e, inner_e = adjoint_local(grad_e, expert_in, target_expert, expert_cols)
    inner_g, inner_e = lax.psum((inner_g, inner_e), ("group", "expert"))
    next_g = adjoint_finish(scaled_g, inner_g, target_group, group_cols)
    next_e = adjoint_finish(scaled_e, inner_e, target_expert, expert_cols)
    return ((next_g, next_e), None)


def deliver(payload):
    halfway = (
        lax.all_to_all(payload[0], "expert", split_axis=1, concat_axis=1, tiled=True),
        lax.all_to_all(payload[1], "expert", split_axis=1, concat_axis=1, tiled=True),
    )
    return (
        lax.all_to_all(halfway[0], "group", split_axis=0, concat_axis=0, tiled=True),
        lax.all_to_all(halfway[1], "group", split_axis=0, concat_axis=0, tiled=True),
    )


def per_device(group_logits, expert_logits, expert_ids, cotangent, hidden_saved, w_down):
    groups = lax.axis_size("group")
    per_group = lax.axis_size("expert")
    experts = groups * per_group
    tokens_here = cotangent.shape[0]
    top_count = expert_ids.shape[1]
    model_width = cotangent.shape[1]
    capacity = hidden_saved.shape[1] // experts
    targets = (float(tokens_here * per_group), float(tokens_here * groups))
    flat_ids = expert_ids.reshape(-1)
    picked = (flat_ids[:, None] == jnp.arange(experts, dtype=jnp.int32)[None, :]).astype(jnp.int32)
    positions = jnp.sum((jnp.cumsum(picked, 0) - picked) * picked, 1)
    slot_index = flat_ids * capacity + positions
    serial = jnp.arange(flat_ids.shape[0], dtype=jnp.int32)
    source_index = jnp.zeros((experts * capacity,), jnp.int32).at[slot_index].set(serial)
    filled = jnp.zeros((experts * capacity,), jnp.int32).at[slot_index].set(1)
    fetched = jnp.take(cotangent, source_index // top_count, axis=0)
    send_rows = jnp.where(filled[:, None] > 0, fetched, jnp.zeros_like(fetched))
    send_rows = send_rows.reshape(groups, per_group, capacity, model_width)
    group_of = expert_ids // per_group
    group_aff = capped(group_logits)
    expert_aff = capped(expert_logits).reshape(tokens_here, groups, per_group)
    (group_prob, expert_prob), stored = lax.scan(
        partial(balance_step, targets), (group_aff, expert_aff), None, length=ITERS
    )
    pick_group = jnp.take_along_axis(group_prob, group_of, 1)
    pick_expert = jnp.take_along_axis(expert_prob.reshape(tokens_here, experts), expert_ids, 1)
    pair_prob = pick_group * pick_expert
    total_prob = jnp.sum(pair_prob, 1, keepdims=True)
    gate_prob = pair_prob / total_prob
    gate_sent = (
        jnp.zeros((experts * capacity,), jnp.bfloat16)
        .at[slot_index]
        .set(gate_prob.astype(jnp.bfloat16).reshape(-1))
    )
    gate_sent = gate_sent.reshape(groups, per_group, capacity)
    routed = (
        group_aff,
        expert_aff,
        stored,
        pick_group,
        pick_expert,
        total_prob,
        gate_prob,
        gate_sent,
    )
    got_rows, got_gates = deliver((send_rows, routed[7]))
    group_aff, expert_aff, stored, pick_group, pick_expert, total_prob, gate_prob, unused_gates = (
        routed
    )
    weight = w_down[0]
    saved_hidden = hidden_saved[0]
    expert_rows = got_rows.reshape(-1, model_width)
    unscaled = lax.dot_general(
        expert_rows, weight, (((1,), (1,)), ((), ())), preferred_element_type=jnp.float32
    )
    slot_grad = jnp.sum(unscaled * saved_hidden.astype(jnp.float32), 1)
    grad_rows = (got_gates.reshape(-1, 1).astype(jnp.float32) * unscaled).astype(jnp.bfloat16)
    hidden_grad = grad_rows[None]
    answers = lax.all_to_all(
        lax.all_to_all(
            slot_grad.reshape(groups, per_group, capacity),
            "group",
            split_axis=0,
            concat_axis=0,
            tiled=True,
        ),
        "expert",
        split_axis=1,
        concat_axis=1,
        tiled=True,
    )
    gate_grad = answers.reshape(-1)[slot_index].reshape(tokens_here, top_count)
    pair_grad = (gate_grad - jnp.sum(gate_prob * gate_grad, 1, keepdims=True)) / total_prob
    group_pick = (
        group_of[:, :, None] == jnp.arange(groups, dtype=jnp.int32)[None, None, :]
    ).astype(jnp.float32)
    seed_group = jnp.sum(group_pick * (pair_grad * pick_expert)[:, :, None], 1)
    expert_pick = (
        expert_ids[:, :, None] == jnp.arange(experts, dtype=jnp.int32)[None, None, :]
    ).astype(jnp.float32)
    seed_expert = jnp.sum(expert_pick * (pair_grad * pick_group)[:, :, None], 1).reshape(
        tokens_here, groups, per_group
    )
    (grad_group, grad_expert), unused = lax.scan(
        partial(adjoint_step, targets), (seed_group, seed_expert), stored, reverse=True
    )
    d_group_logits = grad_group * group_aff * squashing(group_logits)
    d_expert_logits = (grad_expert * expert_aff).reshape(tokens_here, experts) * squashing(
        expert_logits
    )
    return (hidden_grad, d_group_logits, d_expert_logits)


def solution(mesh):
    in_specs = (
        P(("group", "expert"), None),
        P(("group", "expert"), None),
        P(("group", "expert"), None),
        P(("group", "expert"), None),
        P(("group", "expert"), None, None),
        P(("group", "expert"), None, None),
    )
    out_specs = (
        P(("group", "expert"), None, None),
        P(("group", "expert"), None),
        P(("group", "expert"), None),
    )
    return jax.shard_map(
        per_device, mesh=mesh, in_specs=in_specs, out_specs=out_specs, check_vma=False
    )
```

profile of v0, /device:TPU:0, one launch (start us, length us, event | category | flops | bytes accessed | tf_op | source)
XLA Modules:
  0.0 600.4 jit_solution(14312915412681843163)
XLA Ops:
  6.8 4.2 gather_fusion
  10.9 3.6 fusion.16
  14.6 5.3 all-to-all-start.2
  20.3 43.2 %all-to-all-done.2 = bf16[4,8,16,3584]{3,2,0,1:T(8,128)(2,1)} async-done(((bf16[4,8,16,3584]{3,2,0,1:T(8,128)(2,1)}), bf16[4,8,16,3584]{3,2,0,1:T(8,128)(2,1)}, u32[]{:S(2)}, u32[]{:S(2)}) %all-to-all-start.2) | async-done | bytes 3670048 | tf_op jit(solution)/shard_map/all_to_all | solution.py:64
  63.5 4.2 copy.114
  67.6 5.6 all-to-all-start.3
  73.2 264.1 %while.36 = (s32[]{:T(128)}, f32[128,4]{0,1:T(4,128)S(1)}, f32[128,4,8]{0,2,1:T(8,128)S(1)}, f32[5,128,4]{1,2,0:T(4,128)S(1)}, f32[5,128,4,8]{1,3,2,0:T(8,128)S(...) while((s32[]{:T(128)}, f32[128,4]{0,1:T(4,128)S(1)}, ...), condition=%wide.region_10.11_spmd, body=%wide.region_3.10_spmd.sunk | while | flops 15277 | bytes 133133 | solution.py:95
  73.4 100.2 %all-reduce.4 = (f32[4]{0:T(128)S(1)}, f32[4,8]{1,0:T(4,128)S(1)}) all-reduce(f32[4]{0:T(128)S(1)} %reduce_sum.212, f32[4,8]{1,0:T(4,128)S(1)} %reduce_sum.213), channel_id=1, replica_groups=mesh['group'=4,'expert'=8] {'group','expert'}, use_global_device_ids=true, to_apply=%region_5.5 | all-reduce | flops 36 | bytes 288 | tf_op jit(solution)/shard_map/while/body/eval_jaxpr/psum | solution.py:39
  174.4 39.5 %all-reduce.4 = (f32[4]{0:T(128)S(1)}, f32[4,8]{1,0:T(4,128)S(1)}) all-reduce(f32[4]{0:T(128)S(1)} %reduce_sum.212, f32[4,8]{1,0:T(4,128)S(1)} %reduce_sum.213), channel_id=1, replica_groups=mesh['group'=4,'expert'=8] {'group','expert'}, use_global_device_ids=true, to_apply=%region_5.5 | all-reduce | flops 36 | bytes 288 | tf_op jit(solution)/shard_map/while/body/eval_jaxpr/psum | solution.py:39
  214.7 40.5 %all-reduce.4 = (f32[4]{0:T(128)S(1)}, f32[4,8]{1,0:T(4,128)S(1)}) all-reduce(f32[4]{0:T(128)S(1)} %reduce_sum.212, f32[4,8]{1,0:T(4,128)S(1)} %reduce_sum.213), channel_id=1, replica_groups=mesh['group'=4,'expert'=8] {'group','expert'}, use_global_device_ids=true, to_apply=%region_5.5 | all-reduce | flops 36 | bytes 288 | tf_op jit(solution)/shard_map/while/body/eval_jaxpr/psum | solution.py:39
  256.0 39.4 %all-reduce.4 = (f32[4]{0:T(128)S(1)}, f32[4,8]{1,0:T(4,128)S(1)}) all-reduce(f32[4]{0:T(128)S(1)} %reduce_sum.212, f32[4,8]{1,0:T(4,128)S(1)} %reduce_sum.213), channel_id=1, replica_groups=mesh['group'=4,'expert'=8] {'group','expert'}, use_global_device_ids=true, to_apply=%region_5.5 | all-reduce | flops 36 | bytes 288 | tf_op jit(solution)/shard_map/while/body/eval_jaxpr/psum | solution.py:39
  296.1 40.6 %all-reduce.4 = (f32[4]{0:T(128)S(1)}, f32[4,8]{1,0:T(4,128)S(1)}) all-reduce(f32[4]{0:T(128)S(1)} %reduce_sum.212, f32[4,8]{1,0:T(4,128)S(1)} %reduce_sum.213), channel_id=1, replica_groups=mesh['group'=4,'expert'=8] {'group','expert'}, use_global_device_ids=true, to_apply=%region_5.5 | all-reduce | flops 36 | bytes 288 | tf_op jit(solution)/shard_map/while/body/eval_jaxpr/psum | solution.py:39
  342.3 8.4 %fusion.17 = (f32[512]{0:T(512)S(1)}, f32[512,1024]{1,0:T(8,128)S(1)}) fusion(bf16[1,512,1024]{2,1,0:T(8,128)(2,1)} %param.14, bf16[512,3584]{1,0:T(8,128)(2,1)} %bitcast.18, bf16[1,1024,3584]{2,1,0:T(8,128)(2,1)} %param.15), kind=kOutput, calls=%fused_computation.49 | convolution fusion | flops 3759668736 | bytes 14157824 | tf_op jit(solution)/shard_map/dot_general | solution.py:126
  354.9 5.5 all-to-all-done.4
  362.2 4.6 all-to-all-start.5
  366.9 4.7 all-to-all-done.5
  373.9 204.3 %while.37 = (s32[]{:T(128)}, f32[128,4]{0,1:T(4,128)S(1)}, f32[128,4,8]{0,2,1:T(8,128)S(1)}, f32[5,4]{1,0:T(8,128)S(1)}, f32[5,128,4]{1,2,0:T(4,128)S(1)}, /*ind...) while((s32[]{:T(128)}, f32[128,4]{0,1:T(4,128)S(1)}, ...), condition=%wide.region_28.29_spmd, body=%wide.region_19.28_spmd.sunk | while | flops 52050 | bytes 159945 | solution.py:157
  375.0 38.3 %all-reduce.5 = (f32[4]{0:T(128)S(1)}, f32[4,8]{1,0:T(4,128)S(1)}) all-reduce(f32[4]{0:T(128)S(1)} %fusion.48, f32[4,8]{1,0:T(4,128)S(1)} %get-tuple-element.338), channel_id=1, replica_groups=mesh['group'=4,'expert'=8] {'group','expert'}, use_global_device_ids=true, to_apply=%region_23.23 | all-reduce | flops 36 | bytes 288 | tf_op jit(solution)/shard_map/while/body/eval_jaxpr/psum | solution.py:56
  414.5 40.1 %all-reduce.5 = (f32[4]{0:T(128)S(1)}, f32[4,8]{1,0:T(4,128)S(1)}) all-reduce(f32[4]{0:T(128)S(1)} %fusion.48, f32[4,8]{1,0:T(4,128)S(1)} %get-tuple-element.338), channel_id=1, replica_groups=mesh['group'=4,'expert'=8] {'group','expert'}, use_global_device_ids=true, to_apply=%region_23.23 | all-reduce | flops 36 | bytes 288 | tf_op jit(solution)/shard_map/while/body/eval_jaxpr/psum | solution.py:56
  455.8 39.9 %all-reduce.5 = (f32[4]{0:T(128)S(1)}, f32[4,8]{1,0:T(4,128)S(1)}) all-reduce(f32[4]{0:T(128)S(1)} %fusion.48, f32[4,8]{1,0:T(4,128)S(1)} %get-tuple-element.338), channel_id=1, replica_groups=mesh['group'=4,'expert'=8] {'group','expert'}, use_global_device_ids=true, to_apply=%region_23.23 | all-reduce | flops 36 | bytes 288 | tf_op jit(solution)/shard_map/while/body/eval_jaxpr/psum | solution.py:56
  496.9 40.1 %all-reduce.5 = (f32[4]{0:T(128)S(1)}, f32[4,8]{1,0:T(4,128)S(1)}) all-reduce(f32[4]{0:T(128)S(1)} %fusion.48, f32[4,8]{1,0:T(4,128)S(1)} %get-tuple-element.338), channel_id=1, replica_groups=mesh['group'=4,'expert'=8] {'group','expert'}, use_global_device_ids=true, to_apply=%region_23.23 | all-reduce | flops 36 | bytes 288 | tf_op jit(solution)/shard_map/while/body/eval_jaxpr/psum | solution.py:56
  538.3 39.8 %all-reduce.5 = (f32[4]{0:T(128)S(1)}, f32[4,8]{1,0:T(4,128)S(1)}) all-reduce(f32[4]{0:T(128)S(1)} %fusion.48, f32[4,8]{1,0:T(4,128)S(1)} %get-tuple-element.338), channel_id=1, replica_groups=mesh['group'=4,'expert'=8] {'group','expert'}, use_global_device_ids=true, to_apply=%region_23.23 | all-reduce | flops 36 | bytes 288 | tf_op jit(solution)/shard_map/while/body/eval_jaxpr/psum | solution.py:56
  585.6 4.1 all-to-all-done
  594.2 5.0 all-to-all-done.1
  (196 shorter events, 42.5 us)
Async XLA Ops:
  0.6 6.1 %copy-start = (bf16[128,3584]{1,0:T(8,128)(2,1)S(1)}, bf16[128,3584]{1,0:T(8,128)(2,1)}, u32[]{:S(2)}) copy-start(bf16[128,3584]{1,0:T(8,128)(2,1)} %param.13) | copy-start | bytes 2752516
  14.6 5.4 copy-start.2
  14.6 5.7 copy-start.3
  14.6 5.7 copy-start.1
  14.6 48.9 %all-to-all-start.2 = ((bf16[4,8,16,3584]{3,2,0,1:T(8,128)(2,1)}), bf16[4,8,16,3584]{3,2,0,1:T(8,128)(2,1)}, u32[]{:S(2)}, u32[]{:S(2)}) async-start(bf16[4,8,16,3584]{3,2,0,1:T(8,128)(2,1)} %fusion.16), calls=%async_computation.2 | async-start | bytes 7340032 | tf_op jit(solution)/shard_map/all_to_all | solution.py:64
  67.6 274.7 %all-to-all-start.3 = ((bf16[4,8,16,3584]{3,2,1,0:T(8,128)(2,1)}), bf16[4,8,16,3584]{3,2,1,0:T(8,128)(2,1)}, u32[]{:S(2)}, u32[]{:S(2)}) async-start(bf16[4,8,16,3584]{3,2,1,0:T(8,128)(2,1)} %copy.114), calls=%async_computation.3 | async-start | bytes 7340032 | tf_op jit(solution)/shard_map/all_to_all | solution.py:68
  351.5 8.9 %all-to-all-start.4 = ((f32[4,1,128]{2,1,0:T(1,128)}), f32[4,1,128]{2,1,0:T(1,128)S(1)}, u32[]{:S(2)}, u32[]{:S(2)}) async-start(f32[4,1,128]{2,1,0:T(1,128)} %reshape.275), calls=%async_computation.4 | async-start | bytes 4096 | tf_op jit(solution)/shard_map/all_to_all | solution.py:133
  362.2 9.4 %all-to-all-start.5 = ((f32[4,8,16]{2,0,1:T(4,128)}), f32[4,8,16]{2,0,1:T(4,128)S(1)}, u32[]{:S(2)}, u32[]{:S(2)}) async-start(f32[4,8,16]{2,0,1:T(4,128)} %copy.115), calls=%async_computation.5 | async-start | bytes 32768 | tf_op jit(solution)/shard_map/all_to_all | solution.py:132
  581.5 8.3 %all-to-all-start = ((bf16[4,8,16]{2,0,1:T(4,128)(2,1)}), bf16[4,8,16]{2,0,1:T(4,128)(2,1)S(1)}, u32[]{:S(2)}, u32[]{:S(2)}) async-start(bf16[4,8,16]{2,0,1:T(4,128)(2,1)} %copy.109), calls=%async_computation | async-start | bytes 16384 | tf_op jit(solution)/shard_map/all_to_all | solution.py:65
  590.3 8.8 %all-to-all-start.1 = ((bf16[4,8,16]{2,1,0:T(8,128)(2,1)}), bf16[4,8,16]{2,1,0:T(8,128)(2,1)S(1)}, u32[]{:S(2)}, u32[]{:S(2)}) async-start(bf16[4,8,16]{2,1,0:T(8,128)(2,1)} %copy.110), calls=%async_computation.1 | async-start | bytes 16384 | tf_op jit(solution)/shard_map/all_to_all | solution.py:69
where the time goes:
time: 602 us; the launch traced here: 600 us
  blocking collectives  458 us (76%)
  waiting for transfers between devices  62.5 us (10%)
  local copies, waits for them, and re-layouts  26.5 us (4%)
  starting transfers between devices  25.7 us (4%)
  other arithmetic  17.9 us (3%)
  matrix products  8.44 us (1%)
    psum x5, blocking collectives, balance_step(): lax.psum((jnp.sum(group_in, 0), jnp.sum(expert_in, 0)), ('group', 'expert'))  260 us
    psum x5, blocking collectives, adjoint_step(): inner_g, inner_e = lax.psum((inner_g, inner_e), ('group', 'expert'))  198 us
    all_to_all x1, waiting for transfers between devices, deliver(): lax.all_to_all(payload[0], 'expert', split_axis=1, concat_axis=1, tiled=T...  43.2 us
  transfers between devices with their start and end apart: 6, of which 5 were waited for; matrix products, arithmetic and copies ran while one was open for 2% of the time, Pallas kernels for 0%

commit v1 on v0

--- a/solution.py
+++ b/solution.py
@@ -37,7 +37,7 @@
     target_group, target_expert = targets
     group_in, expert_in = current
     group_cols, expert_cols = lax.psum(
-        (jnp.sum(group_in, 0), jnp.sum(expert_in, 0)), ("group", "expert")
+        lax.psum((jnp.sum(group_in, 0), jnp.sum(expert_in, 0)), "expert"), "group"
     )
     scaled_g, rowsum_g = balance_level(group_in, target_group, group_cols)
     scaled_e, rowsum_e = balance_level(expert_in, target_expert, expert_cols)

time: 602 us -> 507 us (0.84)
  blocking collectives: 458 us -> 364 us
    psum x5 -> x10, blocking collectives: 260 us -> 166 us  [the longest x5 105 us: balance_step(): lax.psum(lax.psum((jnp.sum(group_in, 0), jnp.sum(expert_in, 0)), 'expert'...]
where the time goes in v1:
time: 507 us; the launch traced here: 505 us
  blocking collectives  364 us (72%)
  waiting for transfers between devices  62.2 us (12%)
  local copies, waits for them, and re-layouts  26.4 us (5%)
  starting transfers between devices  24.5 us (5%)
  other arithmetic  17.9 us (4%)
  matrix products  8.44 us (2%)
    psum x5, blocking collectives, adjoint_step(): inner_g, inner_e = lax.psum((inner_g, inner_e), ('group', 'expert'))  198 us
    psum x5, blocking collectives, balance_step(): lax.psum(lax.psum((jnp.sum(group_in, 0), jnp.sum(expert_in, 0)), 'expert'...  105 us
    psum x5, blocking collectives, balance_step(): lax.psum((jnp.sum(group_in, 0), jnp.sum(expert_in, 0)), 'expert')  60.9 us
    all_to_all x1, waiting for transfers between devices, deliver(): lax.all_to_all(payload[0], 'expert', split_axis=1, concat_axis=1, tiled=T...  43.2 us
  transfers between devices with their start and end apart: 6, of which 5 were waited for; matrix products, arithmetic and copies ran while one was open for 2% of the time, Pallas kernels for 0%

profile of v1, /device:TPU:0, one launch (start us, length us, event | category | flops | bytes accessed | tf_op | source)
XLA Modules:
  0.0 505.0 jit_solution(6844061879830313497)
XLA Ops:
  14.6 5.3 %all-to-all-start.2 = ((bf16[4,8,16,3584]{3,2,0,1:T(8,128)(2,1)}), bf16[4,8,16,3584]{3,2,0,1:T(8,128)(2,1)}, u32[]{:S(2)}, u32[]{:S(2)}) async-start(bf16[4,8,16,3584]{3,2,0,1:T(8,128)(2,1)} %fusion.16), calls=%async_computation.2 | async-start | bytes 7340032 | tf_op jit(solution)/shard_map/all_to_all | solution.py:64
  20.3 43.2 %all-to-all-done.2 = bf16[4,8,16,3584]{3,2,0,1:T(8,128)(2,1)} async-done(((bf16[4,8,16,3584]{3,2,0,1:T(8,128)(2,1)}), bf16[4,8,16,3584]{3,2,0,1:T(8,128)(2,1)}, u32[]{:S(2)}, u32[]{:S(2)}) %all-to-all-start.2) | async-done | bytes 3670048 | tf_op jit(solution)/shard_map/all_to_all | solution.py:64
  67.6 5.6 %all-to-all-start.3 = ((bf16[4,8,16,3584]{3,2,1,0:T(8,128)(2,1)}), bf16[4,8,16,3584]{3,2,1,0:T(8,128)(2,1)}, u32[]{:S(2)}, u32[]{:S(2)}) async-start(bf16[4,8,16,3584]{3,2,1,0:T(8,128)(2,1)} %copy.114), calls=%async_computation.3 | async-start | bytes 7340032 | tf_op jit(solution)/shard_map/all_to_all | solution.py:68
  73.2 170.2 %while.36 = (s32[]{:T(128)}, f32[128,4]{0,1:T(4,128)S(1)}, f32[128,4,8]{0,2,1:T(8,128)S(1)}, f32[5,128,4]{1,2,0:T(4,128)S(1)}, f32[5,128,4,8]{1,3,2,0:T(8,128)S(...) while((s32[]{:T(128)}, f32[128,4]{0,1:T(4,128)S(1)}, ...), condition=%wide.region_12.13_spmd, body=%wide.region_3.12_spmd.sunk | while | flops 15313 | bytes 133421 | solution.py:95
  73.4 12.2 %all-reduce.6 = (f32[4]{0:T(128)S(1)}, f32[4,8]{1,0:T(4,128)S(1)}) all-reduce(f32[4]{0:T(128)S(1)} %reduce_sum.212, f32[4,8]{1,0:T(4,128)S(1)} %reduce_sum.213), channel_id=1, replica_groups=mesh['group'=4,'expert'=8] {'expert'}, use_global_device_ids=true, to_apply=%region_5.5 | all-reduce | flops 36 | bytes 288 | tf_op jit(solution)/shard_map/while/body/eval_jaxpr/psum | solution.py:40
  85.6 50.0 %all-reduce.7 = (f32[4]{0:T(128)S(1)}, f32[4,8]{1,0:T(4,128)S(1)}) all-reduce(f32[4]{0:T(128)S(1)} %get-tuple-element.333, f32[4,8]{1,0:T(4,128)S(1)} %get-tuple-element.334), channel_id=1, replica_groups=mesh['group'=4,'expert'=8] {'group'}, use_global_device_ids=true, to_apply=%region_6.6 | all-reduce | flops 36 | bytes 288 | tf_op jit(solution)/shard_map/while/body/eval_jaxpr/psum | solution.py:39
  136.4 13.4 %all-reduce.6 = (f32[4]{0:T(128)S(1)}, f32[4,8]{1,0:T(4,128)S(1)}) all-reduce(f32[4]{0:T(128)S(1)} %reduce_sum.212, f32[4,8]{1,0:T(4,128)S(1)} %reduce_sum.213), channel_id=1, replica_groups=mesh['group'=4,'expert'=8] {'expert'}, use_global_device_ids=true, to_apply=%region_5.5 | all-reduce | flops 36 | bytes 288 | tf_op jit(solution)/shard_map/while/body/eval_jaxpr/psum | solution.py:40
  149.8 28.2 %all-reduce.7 = (f32[4]{0:T(128)S(1)}, f32[4,8]{1,0:T(4,128)S(1)}) all-reduce(f32[4]{0:T(128)S(1)} %get-tuple-element.333, f32[4,8]{1,0:T(4,128)S(1)} %get-tuple-element.334), channel_id=1, replica_groups=mesh['group'=4,'expert'=8] {'group'}, use_global_device_ids=true, to_apply=%region_6.6 | all-reduce | flops 36 | bytes 288 | tf_op jit(solution)/shard_map/while/body/eval_jaxpr/psum | solution.py:39
  178.8 11.8 %all-reduce.6 = (f32[4]{0:T(128)S(1)}, f32[4,8]{1,0:T(4,128)S(1)}) all-reduce(f32[4]{0:T(128)S(1)} %reduce_sum.212, f32[4,8]{1,0:T(4,128)S(1)} %reduce_sum.213), channel_id=1, replica_groups=mesh['group'=4,'expert'=8] {'expert'}, use_global_device_ids=true, to_apply=%region_5.5 | all-reduce | flops 36 | bytes 288 | tf_op jit(solution)/shard_map/while/body/eval_jaxpr/psum | solution.py:40
  190.6 8.4 %all-reduce.7 = (f32[4]{0:T(128)S(1)}, f32[4,8]{1,0:T(4,128)S(1)}) all-reduce(f32[4]{0:T(128)S(1)} %get-tuple-element.333, f32[4,8]{1,0:T(4,128)S(1)} %get-tuple-element.334), channel_id=1, replica_groups=mesh['group'=4,'expert'=8] {'group'}, use_global_device_ids=true, to_apply=%region_6.6 | all-reduce | flops 36 | bytes 288 | tf_op jit(solution)/shard_map/while/body/eval_jaxpr/psum | solution.py:39
  199.7 11.8 %all-reduce.6 = (f32[4]{0:T(128)S(1)}, f32[4,8]{1,0:T(4,128)S(1)}) all-reduce(f32[4]{0:T(128)S(1)} %reduce_sum.212, f32[4,8]{1,0:T(4,128)S(1)} %reduce_sum.213), channel_id=1, replica_groups=mesh['group'=4,'expert'=8] {'expert'}, use_global_device_ids=true, to_apply=%region_5.5 | all-reduce | flops 36 | bytes 288 | tf_op jit(solution)/shard_map/while/body/eval_jaxpr/psum | solution.py:40
  211.5 10.4 %all-reduce.7 = (f32[4]{0:T(128)S(1)}, f32[4,8]{1,0:T(4,128)S(1)}) all-reduce(f32[4]{0:T(128)S(1)} %get-tuple-element.333, f32[4,8]{1,0:T(4,128)S(1)} %get-tuple-element.334), channel_id=1, replica_groups=mesh['group'=4,'expert'=8] {'group'}, use_global_device_ids=true, to_apply=%region_6.6 | all-reduce | flops 36 | bytes 288 | tf_op jit(solution)/shard_map/while/body/eval_jaxpr/psum | solution.py:39
  222.7 11.8 %all-reduce.6 = (f32[4]{0:T(128)S(1)}, f32[4,8]{1,0:T(4,128)S(1)}) all-reduce(f32[4]{0:T(128)S(1)} %reduce_sum.212, f32[4,8]{1,0:T(4,128)S(1)} %reduce_sum.213), channel_id=1, replica_groups=mesh['group'=4,'expert'=8] {'expert'}, use_global_device_ids=true, to_apply=%region_5.5 | all-reduce | flops 36 | bytes 288 | tf_op jit(solution)/shard_map/while/body/eval_jaxpr/psum | solution.py:40
  234.5 8.4 %all-reduce.7 = (f32[4]{0:T(128)S(1)}, f32[4,8]{1,0:T(4,128)S(1)}) all-reduce(f32[4]{0:T(128)S(1)} %get-tuple-element.333, f32[4,8]{1,0:T(4,128)S(1)} %get-tuple-element.334), channel_id=1, replica_groups=mesh['group'=4,'expert'=8] {'group'}, use_global_device_ids=true, to_apply=%region_6.6 | all-reduce | flops 36 | bytes 288 | tf_op jit(solution)/shard_map/while/body/eval_jaxpr/psum | solution.py:39
  248.4 8.4 %fusion.17 = (f32[512]{0:T(512)S(1)}, f32[512,1024]{1,0:T(8,128)S(1)}) fusion(bf16[1,512,1024]{2,1,0:T(8,128)(2,1)} %param.14, bf16[512,3584]{1,0:T(8,128)(2,1)} %bitcast.18, bf16[1,1024,3584]{2,1,0:T(8,128)(2,1)} %param.15), kind=kOutput, calls=%fused_computation.49 | convolution fusion | flops 3759668736 | bytes 14157824 | tf_op jit(solution)/shard_map/dot_general | solution.py:126
  260.9 5.5 %all-to-all-done.4 = f32[4,1,128]{2,1,0:T(1,128)S(1)} async-done(((f32[4,1,128]{2,1,0:T(1,128)}), f32[4,1,128]{2,1,0:T(1,128)S(1)}, u32[]{:S(2)}, u32[]{:S(2)}) %all-to-all-start.4) | async-done | bytes 2080 | tf_op jit(solution)/shard_map/all_to_all | solution.py:133
  271.8 4.5 all-to-all-done.5
  278.7 204.3 %while.37 = (s32[]{:T(128)}, f32[128,4]{0,1:T(4,128)S(1)}, f32[128,4,8]{0,2,1:T(8,128)S(1)}, f32[5,4]{1,0:T(8,128)S(1)}, f32[5,128,4]{1,2,0:T(4,128)S(1)}, /*ind...) while((s32[]{:T(128)}, f32[128,4]{0,1:T(4,128)S(1)}, ...), condition=%wide.region_30.31_spmd, body=%wide.region_21.30_spmd.sunk | while | flops 52050 | bytes 159945 | solution.py:157
  279.7 38.3 %all-reduce.8 = (f32[4]{0:T(128)S(1)}, f32[4,8]{1,0:T(4,128)S(1)}) all-reduce(f32[4]{0:T(128)S(1)} %fusion.48, f32[4,8]{1,0:T(4,128)S(1)} %get-tuple-element.344), channel_id=1, replica_groups=mesh['group'=4,'expert'=8] {'group','expert'}, use_global_device_ids=true, to_apply=%region_25.25 | all-reduce | flops 36 | bytes 288 | tf_op jit(solution)/shard_map/while/body/eval_jaxpr/psum | solution.py:56
  319.2 40.0 %all-reduce.8 = (f32[4]{0:T(128)S(1)}, f32[4,8]{1,0:T(4,128)S(1)}) all-reduce(f32[4]{0:T(128)S(1)} %fusion.48, f32[4,8]{1,0:T(4,128)S(1)} %get-tuple-element.344), channel_id=1, replica_groups=mesh['group'=4,'expert'=8] {'group','expert'}, use_global_device_ids=true, to_apply=%region_25.25 | all-reduce | flops 36 | bytes 288 | tf_op jit(solution)/shard_map/while/body/eval_jaxpr/psum | solution.py:56
  360.5 39.9 %all-reduce.8 = (f32[4]{0:T(128)S(1)}, f32[4,8]{1,0:T(4,128)S(1)}) all-reduce(f32[4]{0:T(128)S(1)} %fusion.48, f32[4,8]{1,0:T(4,128)S(1)} %get-tuple-element.344), channel_id=1, replica_groups=mesh['group'=4,'expert'=8] {'group','expert'}, use_global_device_ids=true, to_apply=%region_25.25 | all-reduce | flops 36 | bytes 288 | tf_op jit(solution)/shard_map/while/body/eval_jaxpr/psum | solution.py:56
  401.6 40.1 %all-reduce.8 = (f32[4]{0:T(128)S(1)}, f32[4,8]{1,0:T(4,128)S(1)}) all-reduce(f32[4]{0:T(128)S(1)} %fusion.48, f32[4,8]{1,0:T(4,128)S(1)} %get-tuple-element.344), channel_id=1, replica_groups=mesh['group'=4,'expert'=8] {'group','expert'}, use_global_device_ids=true, to_apply=%region_25.25 | all-reduce | flops 36 | bytes 288 | tf_op jit(solution)/shard_map/while/body/eval_jaxpr/psum | solution.py:56
  442.9 39.8 %all-reduce.8 = (f32[4]{0:T(128)S(1)}, f32[4,8]{1,0:T(4,128)S(1)}) all-reduce(f32[4]{0:T(128)S(1)} %fusion.48, f32[4,8]{1,0:T(4,128)S(1)} %get-tuple-element.344), channel_id=1, replica_groups=mesh['group'=4,'expert'=8] {'group','expert'}, use_global_device_ids=true, to_apply=%region_25.25 | all-reduce | flops 36 | bytes 288 | tf_op jit(solution)/shard_map/while/body/eval_jaxpr/psum | solution.py:56
  498.8 5.0 all-to-all-done.1
  (201 shorter events, 62.0 us)
Async XLA Ops:
  0.6 6.1 %copy-start = (bf16[128,3584]{1,0:T(8,128)(2,1)S(1)}, bf16[128,3584]{1,0:T(8,128)(2,1)}, u32[]{:S(2)}) copy-start(bf16[128,3584]{1,0:T(8,128)(2,1)} %param.13) | copy-start | bytes 2752516
  14.6 5.4 %copy-start.2 = (s32[128,2]{0,1:T(2,128)S(1)}, s32[128,2]{0,1:T(2,128)}, u32[]{:S(2)}) copy-start(s32[128,2]{0,1:T(2,128)} %param.12) | copy-start | bytes 3076
  14.6 5.7 %copy-start.3 = (f32[128,4]{0,1:T(4,128)S(1)}, f32[128,4]{0,1:T(4,128)}, u32[]{:S(2)}) copy-start(f32[128,4]{0,1:T(4,128)} %param.10) | copy-start | bytes 6148
  14.6 5.7 %copy-start.1 = (f32[128,32]{0,1:T(8,128)S(1)}, f32[128,32]{0,1:T(8,128)}, u32[]{:S(2)}) copy-start(f32[128,32]{0,1:T(8,128)} %param.11) | copy-start | bytes 49156
  14.6 48.9 %all-to-all-start.2 = ((bf16[4,8,16,3584]{3,2,0,1:T(8,128)(2,1)}), bf16[4,8,16,3584]{3,2,0,1:T(8,128)(2,1)}, u32[]{:S(2)}, u32[]{:S(2)}) async-start(bf16[4,8,16,3584]{3,2,0,1:T(8,128)(2,1)} %fusion.16), calls=%async_computation.2 | async-start | bytes 7340032 | tf_op jit(solution)/shard_map/all_to_all | solution.py:64
  67.6 180.8 %all-to-all-start.3 = ((bf16[4,8,16,3584]{3,2,1,0:T(8,128)(2,1)}), bf16[4,8,16,3584]{3,2,1,0:T(8,128)(2,1)}, u32[]{:S(2)}, u32[]{:S(2)}) async-start(bf16[4,8,16,3584]{3,2,1,0:T(8,128)(2,1)} %copy.114), calls=%async_computation.3 | async-start | bytes 7340032 | tf_op jit(solution)/shard_map/all_to_all | solution.py:68
  257.6 8.8 %all-to-all-start.4 = ((f32[4,1,128]{2,1,0:T(1,128)}), f32[4,1,128]{2,1,0:T(1,128)S(1)}, u32[]{:S(2)}, u32[]{:S(2)}) async-start(f32[4,1,128]{2,1,0:T(1,128)} %reshape.275), calls=%async_computation.4 | async-start | bytes 4096 | tf_op jit(solution)/shard_map/all_to_all | solution.py:133
  268.3 8.0 %all-to-all-start.5 = ((f32[4,8,16]{2,0,1:T(4,128)}), f32[4,8,16]{2,0,1:T(4,128)S(1)}, u32[]{:S(2)}, u32[]{:S(2)}) async-start(f32[4,8,16]{2,0,1:T(4,128)} %copy.115), calls=%async_computation.5 | async-start | bytes 32768 | tf_op jit(solution)/shard_map/all_to_all | solution.py:132
  486.1 8.3 %all-to-all-start = ((bf16[4,8,16]{2,0,1:T(4,128)(2,1)}), bf16[4,8,16]{2,0,1:T(4,128)(2,1)S(1)}, u32[]{:S(2)}, u32[]{:S(2)}) async-start(bf16[4,8,16]{2,0,1:T(4,128)(2,1)} %copy.109), calls=%async_computation | async-start | bytes 16384 | tf_op jit(solution)/shard_map/all_to_all | solution.py:65
  495.0 8.8 %all-to-all-start.1 = ((bf16[4,8,16]{2,1,0:T(8,128)(2,1)}), bf16[4,8,16]{2,1,0:T(8,128)(2,1)S(1)}, u32[]{:S(2)}, u32[]{:S(2)}) async-start(bf16[4,8,16]{2,1,0:T(8,128)(2,1)} %copy.110), calls=%async_computation.1 | async-start | bytes 16384 | tf_op jit(solution)/shard_map/all_to_all | solution.py:69
